TPU v7x, 32 devices: a whole 2x2x4 slice. The times are simulated.
32 devices in a mesh: fsdp: 2 (over core), context: 4 (over y, x), tensor: 4 (over z).
Axes of the slice: x: 2, y: 2, z: 4, core: 2. Of those that a mesh axis runs over, the one named last changes fastest.
Arguments:
- inputs: bfloat16 [2, 2, 1280, 2048], P(None, 'fsdp', ('context', 'tensor')), may hold values from -6 to 6
- segments: int32 [2, 2, 1280], P(None, 'fsdp'), may hold values from 0 to 7, never falling along the last dimension, each value on 1 to 640 neighbouring positions
- norm_gain: float32 [2048], replicated, may hold values from 0.5 to 1.5
- branch_weight: bfloat16 [2048, 2560], P(('fsdp', 'context'), 'tensor'), may hold values from -0.125 to 0.125
- inner_weight: bfloat16 [2048, 2560], P(('fsdp', 'context'), 'tensor'), may hold values from -0.125 to 0.125
- conv_weight: float32 [4, 2560], P(None, 'tensor'), may hold values from -3 to 3
- conv_bias: float32 [2560], P('tensor'), may hold values from -3 to 3
- rate_weight: bfloat16 [16, 160, 160], P('tensor'), may hold values from -0.5 to 0.5
- rate_bias: float32 [2560], P('tensor'), may hold values from -4 to 4
- input_weight: bfloat16 [16, 160, 160], P('tensor'), may hold values from -0.5 to 0.5
- input_bias: float32 [2560], P('tensor'), may hold values from -4 to 4
- decay_param: float32 [2560], P('tensor'), may hold values from 4 to 11
- out_weight: bfloat16 [2560, 2048], P('tensor', ('fsdp', 'context')), may hold values from -0.5 to 0.5
- mlp_gain: float32 [2048], replicated, may hold values from 0.5 to 1.5
- gate_weight: bfloat16 [2048, 6144], P(('fsdp', 'context'), 'tensor'), may hold values from -0.125 to 0.125
- up_weight: bfloat16 [2048, 6144], P(('fsdp', 'context'), 'tensor'), may hold values from -0.125 to 0.125
- down_weight: bfloat16 [6144, 2048], P('tensor', ('fsdp', 'context')), may hold values from -0.15625 to 0.15625
- cotangent: bfloat16 [2, 2, 1280, 2048], P(None, 'fsdp', ('context', 'tensor')), may hold values from -6 to 6
Outputs:
- block_out: bfloat16 [2, 2, 1280, 2048], P(None, 'fsdp', ('context', 'tensor'))
- input_grad: float32 [2, 2, 1280, 2048], P(None, 'fsdp', ('context', 'tensor'))
- norm_gain_grad: float32 [2048], replicated
- branch_weight_grad: float32 [2048, 2560], P(('fsdp', 'context'), 'tensor')
- inner_weight_grad: float32 [2048, 2560], P(('fsdp', 'context'), 'tensor')
- conv_weight_grad: float32 [4, 2560], P(None, 'tensor')
- conv_bias_grad: float32 [2560], P('tensor')
- rate_weight_grad: float32 [16, 160, 160], P('tensor')
- rate_bias_grad: float32 [2560], P('tensor')
- input_weight_grad: float32 [16, 160, 160], P('tensor')
- input_bias_grad: float32 [2560], P('tensor')
- decay_param_grad: float32 [2560], P('tensor')
- out_weight_grad: float32 [2560, 2048], P('tensor', ('fsdp', 'context'))
- mlp_gain_grad: float32 [2048], replicated
- gate_weight_grad: float32 [2048, 6144], P(('fsdp', 'context'), 'tensor')
- up_weight_grad: float32 [2048, 6144], P(('fsdp', 'context'), 'tensor')
- down_weight_grad: float32 [6144, 2048], P('tensor', ('fsdp', 'context'))
Inputs may be any that keep to these rules, and one draw needn't show every extreme that they name: `segments`: along each sequence the numbers never fall; each document is one run of 1 to 640 positions, every number of 0 to 7 is used in each sequence, and one document of each sequence has exactly 640 positions.
All inputs are finite; a program needn't handle non-finite values.
Results may differ from a plain program's by a relative error of at most 0.014.
Values may be sent and summed in bfloat16 or wider, within the bound.
No kernel may reach another device: no remote copies, remote signals or barrier semaphores. Data moves between devices by JAX's collectives and lax.ppermute only.
A program may use at most 256 MiB of HBM per device.

v0:
```python
from functools import partial
import jax
import jax.numpy as jnp
from jax import lax
from jax.sharding import PartitionSpec as P

CONV = 4
CPOW = 8
EPS = 1e-06


def from_behind(value, axis, by):
    length = lax.axis_size(axis)
    pairs = [(i, i + by) for i in range(length) if 0 <= i + by < length]
    return lax.ppermute(value, axis, pairs)


def rms_norm(values, gain_vec):
    return values * lax.rsqrt(jnp.mean(values * values, axis=-1, keepdims=True) + EPS) * gain_vec


def round_low(values):
    return lax.optimization_barrier(values.astype(jnp.bfloat16)).astype(jnp.float32)


def combine(earlier, following):
    return (earlier[0] * following[0], following[0] * earlier[1] + following[1])


def local_scan(coeffs, offsets):
    return lax.associative_scan(combine, (coeffs, offsets), axis=1)


def gate_terms(rate_pre, input_pre, conv_vals, decay_param, starts):
    log_rate = -CPOW * jax.nn.softplus(-decay_param) * jax.nn.sigmoid(rate_pre)
    decays = jnp.where(starts, 0.0, jnp.exp(log_rate))
    input_scale = jnp.where(starts, 1.0, jnp.sqrt(-jnp.expm1(2.0 * log_rate)))
    return (decays, input_scale * jax.nn.sigmoid(input_pre) * conv_vals)


def gated_unit(gate_pre, up_pre):
    return jax.nn.gelu(gate_pre) * up_pre


def conv_mix(extended, conv_w, conv_b, same_masks):
    length_rows = extended.shape[1] - (CONV - 1)
    total = conv_b + conv_w[0] * extended[:, CONV - 1 :]
    for offset in range(1, CONV):
        total = (
            total
            + conv_w[offset]
            * extended[:, CONV - 1 - offset : CONV - 1 - offset + length_rows]
            * same_masks[offset - 1]
        )
    return total


def project(rows_in, weight):
    return jnp.einsum("sla,ab->slb", rows_in, weight, preferred_element_type=jnp.float32)


def project_back(grad_vals, weight):
    return jnp.einsum("slb,ab->sla", grad_vals, weight, preferred_element_type=jnp.float32)


def outer_sum(rows_in, grad_vals):
    return jnp.einsum("sla,slb->ab", rows_in, grad_vals, preferred_element_type=jnp.float32)


def split_blocks(values, weight):
    return values.reshape(values.shape[0], values.shape[1], weight.shape[0], weight.shape[1])


def block_mix(values, weight):
    return jnp.einsum(
        "slnb,nbc->slnc", split_blocks(values, weight), weight, preferred_element_type=jnp.float32
    ).reshape(values.shape)


def block_back(grad_vals, weight):
    return jnp.einsum(
        "slnc,nbc->slnb",
        split_blocks(grad_vals, weight),
        weight,
        preferred_element_type=jnp.float32,
    ).reshape(grad_vals.shape)


def block_outer(values, grad_vals, weight):
    return jnp.einsum(
        "slnb,slnc->nbc",
        split_blocks(values, weight),
        split_blocks(grad_vals, weight),
        preferred_element_type=jnp.float32,
    )


def fetch_weights(branch_w, inner_w, gate_w, up_w, out_w, down_w):
    return (
        lax.all_gather(branch_w, ("fsdp", "context"), axis=0, tiled=True),
        lax.all_gather(inner_w, ("fsdp", "context"), axis=0, tiled=True),
        lax.all_gather(gate_w, ("fsdp", "context"), axis=0, tiled=True),
        lax.all_gather(up_w, ("fsdp", "context"), axis=0, tiled=True),
        lax.all_gather(out_w, ("fsdp", "context"), axis=1, tiled=True),
        lax.all_gather(down_w, ("fsdp", "context"), axis=1, tiled=True),
    )


def widen_rows(values):
    return lax.all_gather(values, "tensor", axis=1, tiled=True)


def narrow_rows(partial_vals):
    return lax.psum_scatter(partial_vals, "tensor", scatter_dimension=1, tiled=True)


def widen_grads(values):
    return lax.all_gather(values, "tensor", axis=1, tiled=True)


def narrow_grads(partial_vals):
    return lax.psum_scatter(partial_vals, "tensor", scatter_dimension=1, tiled=True)


def carry_state(coeffs, offsets, reverse):
    incoming = jnp.zeros_like(offsets)
    direction = -1 if reverse else 1
    for relay_turn in range(lax.axis_size("context") - 1):
        incoming = from_behind(coeffs * incoming + offsets, "context", direction)
    return incoming


def per_device(
    inputs,
    segments,
    norm_gain,
    branch_weight,
    inner_weight,
    conv_weight,
    conv_bias,
    rate_weight,
    rate_bias,
    input_weight,
    input_bias,
    decay_param,
    out_weight,
    mlp_gain,
    gate_weight,
    up_weight,
    down_weight,
    cotangent,
):
    seq_count = inputs.shape[1]
    span_rows = inputs.shape[2] * lax.axis_size("tensor")
    context_pos = lax.axis_index("context")
    halo_rows = CONV - 1
    lead_pad = jnp.full((seq_count, halo_rows), -1, jnp.int32)
    totals = None
    block_outs = []
    input_grads = []
    for micro_idx in range(inputs.shape[0]):
        gathered = fetch_weights(
            branch_weight, inner_weight, gate_weight, up_weight, out_weight, down_weight
        )
        full_branch, full_inner, full_gate, full_up, full_out, full_down = gathered
        seg_ext = lax.dynamic_slice_in_dim(
            jnp.concatenate([lead_pad, segments[micro_idx]], axis=1),
            context_pos * span_rows,
            span_rows + halo_rows,
            axis=1,
        )
        current = seg_ext[:, halo_rows:]
        same_masks = [
            (seg_ext[:, halo_rows - offset : halo_rows - offset + span_rows] == current).astype(
                jnp.float32
            )[:, :, None]
            for offset in range(1, CONV)
        ]
        starts = (seg_ext[:, halo_rows - 1 : halo_rows - 1 + span_rows] != current)[:, :, None]
        x_rows = inputs[micro_idx].astype(jnp.float32)
        normed_one, norm_one_back = jax.vjp(rms_norm, x_rows, norm_gain)
        wide_one = widen_rows(normed_one.astype(jnp.bfloat16))
        branch_pre = project(wide_one, full_branch)
        inner_low = project(wide_one, full_inner).astype(jnp.bfloat16)
        edge_rows = from_behind(inner_low[:, span_rows - halo_rows :], "context", 1)
        extended = jnp.concatenate([edge_rows, inner_low], axis=1).astype(jnp.float32)
        conv_out, conv_back = jax.vjp(
            partial(conv_mix, same_masks=same_masks), extended, conv_weight, conv_bias
        )
        conv_low = conv_out.astype(jnp.bfloat16)
        rate_pre = block_mix(conv_low, rate_weight) + rate_bias
        input_pre = block_mix(conv_low, input_weight) + input_bias
        (decays, drives), gate_back = jax.vjp(
            partial(gate_terms, starts=starts),
            rate_pre,
            input_pre,
            conv_low.astype(jnp.float32),
            decay_param,
        )
        prod_loc, state_loc = local_scan(decays, drives)
        state_in = carry_state(prod_loc[:, -1], state_loc[:, -1], False)
        states = state_loc + prod_loc * state_in[:, None]
        gelu_branch, gelu_back = jax.vjp(jax.nn.gelu, branch_pre)
        mixed_low = (states * gelu_branch).astype(jnp.bfloat16)
        residual = x_rows + narrow_rows(project(mixed_low, full_out))
        normed_two, norm_two_back = jax.vjp(rms_norm, residual, mlp_gain)
        wide_two = widen_rows(normed_two.astype(jnp.bfloat16))
        gate_pre = project(wide_two, full_gate)
        up_pre = project(wide_two, full_up)
        hidden_val, hidden_back = jax.vjp(gated_unit, gate_pre, up_pre)
        hidden_low = hidden_val.astype(jnp.bfloat16)
        block_outs.append(
            (residual + narrow_rows(project(hidden_low, full_down))).astype(jnp.bfloat16)
        )
        out_grad = cotangent[micro_idx].astype(jnp.float32)
        wide_grad = widen_grads(cotangent[micro_idx])
        down_term = outer_sum(hidden_low, wide_grad)
        gate_grad, up_grad = hidden_back(project_back(wide_grad, full_down))
        gate_low = gate_grad.astype(jnp.bfloat16)
        up_low = up_grad.astype(jnp.bfloat16)
        gate_term = outer_sum(wide_two, gate_low)
        up_term = outer_sum(wide_two, up_low)
        normed_two_grad = round_low(
            narrow_grads(project_back(gate_low, full_gate) + project_back(up_low, full_up))
        )
        resid_norm_grad, gain_two_term = norm_two_back(normed_two_grad)
        resid_grad = out_grad + resid_norm_grad
        wide_resid = widen_grads(resid_grad.astype(jnp.bfloat16))
        out_term = outer_sum(mixed_low, wide_resid)
        mixed_grad = project_back(wide_resid, full_out)
        (branch_grad,) = gelu_back(mixed_grad * states)
        branch_low = branch_grad.astype(jnp.bfloat16)
        state_grad = mixed_grad * gelu_branch
        next_decays = jnp.concatenate([decays[:, 1:], jnp.ones_like(decays[:, :1])], axis=1)
        rev_prod, rev_grad = local_scan(jnp.flip(next_decays, 1), jnp.flip(state_grad, 1))
        rev_prod = jnp.flip(rev_prod, 1)
        rev_grad = jnp.flip(rev_grad, 1)
        grad_in = carry_state(decays[:, 0] * rev_prod[:, 0], decays[:, 0] * rev_grad[:, 0], True)
        drive_grad = rev_grad + rev_prod * grad_in[:, None]
        prev_states = jnp.concatenate([state_in[:, None], states[:, :-1]], axis=1)
        rate_grad, input_pre_grad, conv_part, decay_term = gate_back(
            (drive_grad * prev_states, drive_grad)
        )
        rate_low = rate_grad.astype(jnp.bfloat16)
        input_low = input_pre_grad.astype(jnp.bfloat16)
        rate_w_term = block_outer(conv_low, rate_low, rate_weight)
        rate_b_term = jnp.sum(rate_low.astype(jnp.float32), axis=(0, 1))
        input_w_term = block_outer(conv_low, input_low, input_weight)
        input_b_term = jnp.sum(input_low.astype(jnp.float32), axis=(0, 1))
        conv_grad = (
            conv_part + block_back(rate_low, rate_weight) + block_back(input_low, input_weight)
        )
        ext_grad, conv_w_term, conv_b_term = conv_back(conv_grad)
        edge_grad = from_behind(ext_grad[:, :halo_rows], "context", -1)
        inner_grad = ext_grad[:, halo_rows:] + jnp.concatenate(
            [jnp.zeros_like(ext_grad[:, 2 * halo_rows :]), edge_grad], axis=1
        )
        inner_low_grad = inner_grad.astype(jnp.bfloat16)
        inner_term = outer_sum(wide_one, inner_low_grad)
        branch_term = outer_sum(wide_one, branch_low)
        normed_one_grad = round_low(
            narrow_grads(
                project_back(inner_low_grad, full_inner) + project_back(branch_low, full_branch)
            )
        )
        x_norm_grad, gain_one_term = norm_one_back(normed_one_grad)
        input_grads.append(resid_grad + x_norm_grad)
        terms = (
            gain_one_term,
            branch_term,
            inner_term,
            conv_w_term,
            conv_b_term,
            rate_w_term,
            rate_b_term,
            input_w_term,
            input_b_term,
            decay_term,
            out_term,
            gain_two_term,
            gate_term,
            up_term,
            down_term,
        )
        totals = terms if totals is None else jax.tree.map(jnp.add, totals, terms)
    big_grads = (
        lax.psum_scatter(
            totals[1].astype(jnp.bfloat16), ("fsdp", "context"), scatter_dimension=0, tiled=True
        ).astype(jnp.float32),
        lax.psum_scatter(
            totals[2].astype(jnp.bfloat16), ("fsdp", "context"), scatter_dimension=0, tiled=True
        ).astype(jnp.float32),
        lax.psum_scatter(
            totals[12].astype(jnp.bfloat16), ("fsdp", "context"), scatter_dimension=0, tiled=True
        ).astype(jnp.float32),
        lax.psum_scatter(
            totals[13].astype(jnp.bfloat16), ("fsdp", "context"), scatter_dimension=0, tiled=True
        ).astype(jnp.float32),
        lax.psum_scatter(
            totals[10].astype(jnp.bfloat16), ("fsdp", "context"), scatter_dimension=1, tiled=True
        ).astype(jnp.float32),
        lax.psum_scatter(
            totals[14].astype(jnp.bfloat16), ("fsdp", "context"), scatter_dimension=1, tiled=True
        ).astype(jnp.float32),
    )
    small_grads = (
        lax.psum(totals[3].astype(jnp.bfloat16), ("fsdp", "context")).astype(jnp.float32),
        lax.psum(totals[4].astype(jnp.bfloat16), ("fsdp", "context")).astype(jnp.float32),
        lax.psum(totals[5].astype(jnp.bfloat16), ("fsdp", "context")).astype(jnp.float32),
        lax.psum(totals[6].astype(jnp.bfloat16), ("fsdp", "context")).astype(jnp.float32),
        lax.psum(totals[7].astype(jnp.bfloat16), ("fsdp", "context")).astype(jnp.float32),
        lax.psum(totals[8].astype(jnp.bfloat16), ("fsdp", "context")).astype(jnp.float32),
        lax.psum(totals[9].astype(jnp.bfloat16), ("fsdp", "context")).astype(jnp.float32),
    )
    gain_grads = lax.psum((totals[0], totals[11]), ("fsdp", "context", "tensor"))
    return (
        jnp.stack(block_outs),
        jnp.stack(input_grads),
        gain_grads[0],
        big_grads[0],
        big_grads[1],
        small_grads[0],
        small_grads[1],
        small_grads[2],
        small_grads[3],
        small_grads[4],
        small_grads[5],
        small_grads[6],
        big_grads[4],
        gain_grads[1],
        big_grads[2],
        big_grads[3],
        big_grads[5],
    )


def solution(mesh):
    placed = (
        P(None, "fsdp", ("context", "tensor"), None),
        P(None, "fsdp", None),
        P(),
        P(("fsdp", "context"), "tensor"),
        P(("fsdp", "context"), "tensor"),
        P(None, "tensor"),
        P("tensor"),
        P("tensor", None, None),
        P("tensor"),
        P("tensor", None, None),
        P("tensor"),
        P("tensor"),
        P("tensor", ("fsdp", "context")),
        P(),
        P(("fsdp", "context"), "tensor"),
        P(("fsdp", "context"), "tensor"),
        P("tensor", ("fsdp", "context")),
        P(None, "fsdp", ("context", "tensor"), None),
    )
    return jax.shard_map(
        per_device,
        mesh=mesh,
        in_specs=placed,
        out_specs=(
            P(None, "fsdp", ("context", "tensor"), None),
            P(None, "fsdp", ("context", "tensor"), None),
            P(),
            P(("fsdp", "context"), "tensor"),
            P(("fsdp", "context"), "tensor"),
            P(None, "tensor"),
            P("tensor"),
            P("tensor", None, None),
            P("tensor"),
            P("tensor", None, None),
            P("tensor"),
            P("tensor"),
            P("tensor", ("fsdp", "context")),
            P(),
            P(("fsdp", "context"), "tensor"),
            P(("fsdp", "context"), "tensor"),
            P("tensor", ("fsdp", "context")),
        ),
        check_vma=False,
    )
```

profile of v0, /device:TPU:0, one launch (start us, length us, event | category | flops | bytes accessed | tf_op | source)
XLA Modules:
  0.0 2164.8 jit_solution(8397309703831230440)
XLA Ops:
  14.8 32.1 %all-gather.17.cloned.1.call-done = bf16[1,320,2048]{2,1,0:T(8,128)(2,1)} async-done(((bf16[1,80,2048]{2,1,0:T(8,128)(2,1)}), bf16[1,320,2048]{2,1,0:T(8,128)(2,1)}) %all-gather.17.cloned.1.call-update) | async-done | bytes 1310736 | tf_op jit(solution)/shard_map/all_gather | solution.py:110
  46.9 31.0 %all-gather.19.cloned.1.call-done = bf16[2048,640]{1,0:T(8,128)(2,1)} async-done(((bf16[256,640]{1,0:T(8,128)(2,1)}), bf16[2048,640]{1,0:T(8,128)(2,1)}) %all-gather.19.cloned.1.call-update) | async-done | bytes 2621456 | tf_op jit(solution)/shard_map/all_gather | solution.py:101
  84.8 28.0 %all-gather.33.cloned.1.call-done = bf16[1,320,2048]{2,1,0:T(8,128)(2,1)} async-done(((bf16[1,80,2048]{2,1,0:T(8,128)(2,1)}), bf16[1,320,2048]{2,1,0:T(8,128)(2,1)}) %all-gather.33.cloned.1.call-update) | async-done | bytes 1310736 | tf_op jit(solution)/shard_map/all_gather | solution.py:110
  119.6 24.2 %all-gather.21.cloned.1.call-done = bf16[2048,640]{1,0:T(8,128)(2,1)} async-done(((bf16[256,640]{1,0:T(8,128)(2,1)}), bf16[2048,640]{1,0:T(8,128)(2,1)}) %all-gather.21.cloned.1.call-update) | async-done | bytes 2621456 | tf_op jit(solution)/shard_map/all_gather | solution.py:100
  479.3 51.8 %reduce-scatter.19.cloned.1.call-done = f32[1,80,2048]{2,1,0:T(8,128)} async-done(((f32[1,320,2048]{2,1,0:T(8,128)}), f32[1,80,2048]{2,1,0:T(8,128)}) %reduce-scatter.19.cloned.1.call-update) | async-done | bytes 655376 | tf_op jit(solution)/shard_map/reduce_scatter | solution.py:114
  537.4 40.8 %all-gather.27.cloned.1.call-done = bf16[2048,1536]{1,0:T(8,128)(2,1)} async-done(((bf16[256,1536]{1,0:T(8,128)(2,1)}), bf16[2048,1536]{1,0:T(8,128)(2,1)}) %all-gather.27.cloned.1.call-update) | async-done | bytes 6291472 | tf_op jit(solution)/shard_map/all_gather | solution.py:102
  578.2 34.9 %all-gather.25.cloned.1.call-done = bf16[1,320,2048]{2,1,0:T(8,128)(2,1)} async-done(((bf16[1,80,2048]{2,1,0:T(8,128)(2,1)}), bf16[1,320,2048]{2,1,0:T(8,128)(2,1)}) %all-gather.25.cloned.1.call-update) | async-done | bytes 1310736 | tf_op jit(solution)/shard_map/all_gather | solution.py:110
  613.1 6.7 fusion.51
  619.8 39.6 %all-gather.29.cloned.1.call-done = bf16[2048,1536]{1,0:T(8,128)(2,1)} async-done(((bf16[256,1536]{1,0:T(8,128)(2,1)}), bf16[2048,1536]{1,0:T(8,128)(2,1)}) %all-gather.29.cloned.1.call-update) | async-done | bytes 6291472 | tf_op jit(solution)/shard_map/all_gather | solution.py:103
  659.4 6.7 fusion.49
  666.0 28.2 %all-gather.41.cloned.1.call-done = bf16[1,1,320,2048]{3,2,1,0:T(8,128)(2,1)} async-done(((bf16[1,1,80,2048]{3,2,1,0:T(8,128)(2,1)}), bf16[1,1,320,2048]{3,2,1,0:T(8,128)(2,1)}) %all-gather.41.cloned.1.call-update) | async-done | bytes 1310736 | tf_op jit(solution)/shard_map/all_gather | solution.py:118
  694.2 47.4 %all-gather.31.cloned.1.call-done = bf16[1536,2048]{1,0:T(8,128)(2,1)} async-done(((bf16[1536,256]{1,0:T(8,128)(2,1)}), bf16[1536,2048]{1,0:T(8,128)(2,1)}) %all-gather.31.cloned.1.call-update) | async-done | bytes 6291472 | tf_op jit(solution)/shard_map/all_gather | solution.py:105
  741.7 9.0 multiply_convert_fusion.1
  750.6 5.8 fusion.252
  760.5 52.0 %reduce-scatter.23.cloned.1.call-done = f32[1,80,2048]{2,1,0:T(8,128)} async-done(((f32[1,320,2048]{2,1,0:T(8,128)}), f32[1,80,2048]{2,1,0:T(8,128)}) %reduce-scatter.23.cloned.1.call-update) | async-done | bytes 655376 | tf_op jit(solution)/shard_map/reduce_scatter | solution.py:122
  817.8 31.9 %all-gather.35.cloned.1.call-done = bf16[1,320,2048]{2,1,0:T(8,128)(2,1)} async-done(((bf16[1,80,2048]{2,1,0:T(8,128)(2,1)}), bf16[1,320,2048]{2,1,0:T(8,128)(2,1)}) %all-gather.35.cloned.1.call-update) | async-done | bytes 1310736 | tf_op jit(solution)/shard_map/all_gather | solution.py:110
  849.6 6.8 fusion.36
  856.4 6.5 fusion.34
  863.0 20.4 all-gather.43.cloned.1.call-done
  883.4 8.9 multiply_convert_fusion
  892.2 5.7 fusion.253
  897.9 6.5 fusion.2
  904.6 6.9 convolution_bitcast_fusion
  911.5 44.2 %reduce-scatter.27.cloned.1.call-done = f32[1,80,2048]{2,1,0:T(8,128)} async-done(((f32[1,320,2048]{2,1,0:T(8,128)}), f32[1,80,2048]{2,1,0:T(8,128)}) %reduce-scatter.27.cloned.1.call-update) | async-done | bytes 655376 | tf_op jit(solution)/shard_map/reduce_scatter | solution.py:122
  959.5 50.2 %reduce-scatter.21.cloned.1.call-done = f32[1,80,2048]{2,1,0:T(8,128)} async-done(((f32[1,320,2048]{2,1,0:T(8,128)}), f32[1,80,2048]{2,1,0:T(8,128)}) %reduce-scatter.21.cloned.1.call-update) | async-done | bytes 655376 | tf_op jit(solution)/shard_map/reduce_scatter | solution.py:114
  1036.5 5.7 slice.1250
  1053.5 5.7 slice.1334
  1064.8 5.6 slice.1336
  1088.6 5.6 slice.1254
  1343.9 5.7 slice.1311
  1443.5 5.7 slice.1395
  1490.2 9.6 fusion.47
  1504.4 8.2 rev.17
  1512.6 8.1 rev.18
  1520.7 8.2 rev.19
  1528.9 8.1 rev.20
  1557.7 11.4 add_convert_fusion.2
  1660.1 6.6 convolution_bitcast_fusion.1
  1667.6 28.4 %all-reduce.153 = (bf16[4,640]{1,0:T(4,128)(2,1)S(1)}, bf16[640]{0:T(1024)(128)(2,1)S(1)}, bf16[640]{0:T(1024)(128)(2,1)S(1)}, bf16[640]{0:T(1024)(128)(2,1)S(1)}, bf16[640]{0:T(1024)(128)(2,1)S(1)}) all-reduce(bf16[4,640]{1,0:T(4,128)(2,1)S(1)} %add_convert_fusion.10, ...), channel_id=1, replica_groups=mesh['fsdp'=2,'context'=4,'tensor'=4] {'fsdp','context'}, use_global_device_ids=true, to_apply=%region_29.31 | all-reduce | flops 5120 | bytes 20480 | tf_op jit(solution)/shard_map/psum | solution.py:307
  1705.2 40.2 %reduce-scatter.39.cloned.1.call-done = bf16[256,1536]{1,0:T(8,128)(2,1)} async-done(((bf16[2048,1536]{1,0:T(8,128)(2,1)}), bf16[256,1536]{1,0:T(8,128)(2,1)}) %reduce-scatter.39.cloned.1.call-update) | async-done | bytes 786448 | tf_op jit(solution)/shard_map/reduce_scatter | solution.py:296
  1747.9 63.1 %reduce-scatter.41.cloned.1.call-done = bf16[1536,256]{1,0:T(8,128)(2,1)} async-done(((bf16[1536,2048]{1,0:T(8,128)(2,1)}), bf16[1536,256]{1,0:T(8,128)(2,1)}) %reduce-scatter.41.cloned.1.call-update) | async-done | bytes 786448 | tf_op jit(solution)/shard_map/reduce_scatter | solution.py:302
  1813.3 44.5 %reduce-scatter.31.cloned.1.call-done = bf16[256,640]{1,0:T(8,128)(2,1)} async-done(((bf16[2048,640]{1,0:T(8,128)(2,1)}), bf16[256,640]{1,0:T(8,128)(2,1)}) %reduce-scatter.31.cloned.1.call-update) | async-done | bytes 327696 | tf_op jit(solution)/shard_map/reduce_scatter | solution.py:287
  1859.7 45.1 %reduce-scatter.35.cloned.1.call-done = bf16[640,256]{1,0:T(8,128)(2,1)} async-done(((bf16[640,2048]{1,0:T(8,128)(2,1)}), bf16[640,256]{1,0:T(8,128)(2,1)}) %reduce-scatter.35.cloned.1.call-update) | async-done | bytes 327696 | tf_op jit(solution)/shard_map/reduce_scatter | solution.py:299
  1906.7 45.0 %reduce-scatter.33.cloned.1.call-done = bf16[256,640]{1,0:T(8,128)(2,1)} async-done(((bf16[2048,640]{1,0:T(8,128)(2,1)}), bf16[256,640]{1,0:T(8,128)(2,1)}) %reduce-scatter.33.cloned.1.call-update) | async-done | bytes 327696 | tf_op jit(solution)/shard_map/reduce_scatter | solution.py:290
  1953.5 52.4 %reduce-scatter.25.cloned.1.call-done = f32[1,80,2048]{2,1,0:T(8,128)} async-done(((f32[1,320,2048]{2,1,0:T(8,128)}), f32[1,80,2048]{2,1,0:T(8,128)}) %reduce-scatter.25.cloned.1.call-update) | async-done | bytes 655376 | tf_op jit(solution)/shard_map/reduce_scatter | solution.py:122
  2007.8 52.2 %reduce-scatter.29.cloned.1.call-done = f32[1,80,2048]{2,1,0:T(8,128)} async-done(((f32[1,320,2048]{2,1,0:T(8,128)}), f32[1,80,2048]{2,1,0:T(8,128)}) %reduce-scatter.29.cloned.1.call-update) | async-done | bytes 655376 | tf_op jit(solution)/shard_map/reduce_scatter | solution.py:122
  2065.1 49.0 %reduce-scatter.17.cloned.1.call-done = f32[1,80,2048]{2,1,0:T(8,128)} async-done(((f32[1,320,2048]{2,1,0:T(8,128)}), f32[1,80,2048]{2,1,0:T(8,128)}) %reduce-scatter.17.cloned.1.call-update) | async-done | bytes 655376 | tf_op jit(solution)/shard_map/reduce_scatter | solution.py:114
  2118.0 40.0 %all-reduce.152 = (f32[2048]{0:T(1024)}, f32[2048]{0:T(1024)}) all-reduce(f32[2048]{0:T(1024)S(1)} %add.1474, f32[2048]{0:T(1024)S(1)} %add.1485), channel_id=1, replica_groups=mesh['fsdp'=2,'context'=4,'tensor'=4] {'fsdp','context','tensor'}, use_global_device_ids=true, to_apply=%region_18.20 | all-reduce | flops 4096 | bytes 32768 | tf_op jit(solution)/shard_map/psum | solution.py:315
  (1199 shorter events, 966.8 us)
Async XLA Ops:
  7.2 39.7 %all-gather.17.cloned.1.call-start = ((), (), s32[]{:S(2)}) async-start(), calls=%async_computation.14 | async-start | bytes 1638400 | tf_op jit(solution)/shard_map/all_gather | solution.py:110
  11.4 66.6 %all-gather.19.cloned.1.call-start = ((), (), s32[]{:S(2)}) async-start(), calls=%async_computation.15 | async-start | bytes 2949120 | tf_op jit(solution)/shard_map/all_gather | solution.py:101
  12.1 100.7 %all-gather.33.cloned.1.call-start = ((), (), s32[]{:S(2)}) async-start(), calls=%async_computation.24 | async-start | bytes 1638400 | tf_op jit(solution)/shard_map/all_gather | solution.py:110
  12.9 130.8 %all-gather.21.cloned.1.call-start = ((), (), s32[]{:S(2)}) async-start(), calls=%async_computation.16 | async-start | bytes 2949120 | tf_op jit(solution)/shard_map/all_gather | solution.py:100
  13.5 391.9 %all-gather.23.cloned.1.call-start = ((), (), s32[]{:S(2)}) async-start(), calls=%async_computation.17 | async-start | bytes 2949120 | tf_op jit(solution)/shard_map/all_gather | solution.py:104
  14.0 465.2 %reduce-scatter.15.cloned.1.call-start = ((), (), s32[]{:S(2)}) async-start(), calls=%async_computation.18 | async-start | bytes 3276800 | tf_op jit(solution)/shard_map/reduce_scatter | solution.py:114
  81.3 66.2 %collective-permute-start = (bf16[1,3,640]{2,1,0:T(4,128)(2,1)S(1)}, bf16[1,3,640]{2,1,0:T(4,128)(2,1)S(1)}, u32[]{:S(2)}, u32[]{:S(2)}) collective-permute-start(bf16[1,3,640]{2,1,0:T(4,128)(2,1)S(1)} %slice.1414), channel_id=1, source_target_pairs={{0,4},{4,8},{8,12},{1,5},{5,9},{9,13},{2,6},{6,10},{10,14},{3,7},{... | collective-permute-start | bytes 11528 | tf_op jit(solution)/shard_map/ppermute | solution.py:15
  116.2 31.5 %collective-permute-start.4 = (bf16[1,3,640]{2,1,0:T(4,128)(2,1)S(1)}, bf16[1,3,640]{2,1,0:T(4,128)(2,1)S(1)}, u32[]{:S(2)}, u32[]{:S(2)}) collective-permute-start(bf16[1,3,640]{2,1,0:T(4,128)(2,1)S(1)} %slice.1465), channel_id=1, source_target_pairs={{0,4},{4,8},{8,12},{1,5},{5,9},{9,13},{2,6},{6,10},{10,14},{3,7},{... | collective-permute-start | bytes 11528 | tf_op jit(solution)/shard_map/ppermute | solution.py:15
  156.9 1385.0 %copy-start.5 = (f32[1,320,640]{2,1,0:T(8,128)}, f32[1,320,640]{2,1,0:T(8,128)S(1)}, u32[]{:S(2)}) copy-start(f32[1,320,640]{2,1,0:T(8,128)S(1)} %copy.70) | copy-start | bytes 2457604
  340.7 8.9 collective-permute-start.1
  350.9 10.0 collective-permute-start.2
  362.2 39.7 %collective-permute-start.3 = (f32[1,640]{1,0:T(1,128)}, f32[1,640]{1,0:T(1,128)S(1)}, u32[]{:S(2)}, u32[]{:S(2)}) collective-permute-start(f32[1,640]{1,0:T(1,128)} %multiply_add_fusion.45), channel_id=1, source_target_pairs={{0,4},{4,8},{8,12},{1,5},{5,9},{9,13},{2,6},{6,10},{10,14},{3,7},{... | collective-permute-start | bytes 7688 | tf_op jit(solution)/shard_map/ppermute | solution.py:15
  410.2 120.9 %reduce-scatter.19.cloned.1.call-start = ((), (), s32[]{:S(2)}) async-start(), calls=%async_computation.25 | async-start | bytes 3276800 | tf_op jit(solution)/shard_map/reduce_scatter | solution.py:114
  452.6 3.2 collective-permute-start.5
  456.6 5.5 collective-permute-start.6
  462.8 8.6 collective-permute-start.7
  478.5 99.7 %all-gather.27.cloned.1.call-start = ((), (), s32[]{:S(2)}) async-start(), calls=%async_computation.20 | async-start | bytes 7077888 | tf_op jit(solution)/shard_map/all_gather | solution.py:102
  479.2 133.9 %all-gather.25.cloned.1.call-start = ((), (), s32[]{:S(2)}) async-start(), calls=%async_computation.19 | async-start | bytes 1638400 | tf_op jit(solution)/shard_map/all_gather | solution.py:110
  533.5 476.2 %copy-start.206 = (f32[80]{0:T(128)}, f32[80]{0:T(128)S(1)}, u32[]{:S(2)}) copy-start(f32[80]{0:T(128)S(1)} %fusion.194) | copy-start | bytes 964
  535.2 124.2 %all-gather.29.cloned.1.call-start = ((), (), s32[]{:S(2)}) async-start(), calls=%async_computation.21 | async-start | bytes 7077888 | tf_op jit(solution)/shard_map/all_gather | solution.py:103
  535.8 158.4 %all-gather.41.cloned.1.call-start = ((), (), s32[]{:S(2)}) async-start(), calls=%async_computation.40 | async-start | bytes 1638400 | tf_op jit(solution)/shard_map/all_gather | solution.py:118
  536.7 204.9 %all-gather.31.cloned.1.call-start = ((), (), s32[]{:S(2)}) async-start(), calls=%async_computation.22 | async-start | bytes 7077888 | tf_op jit(solution)/shard_map/all_gather | solution.py:105
  537.3 275.2 %reduce-scatter.23.cloned.1.call-start = ((), (), s32[]{:S(2)}) async-start(), calls=%async_computation.28 | async-start | bytes 3276800 | tf_op jit(solution)/shard_map/reduce_scatter | solution.py:122
  760.2 89.4 %all-gather.35.cloned.1.call-start = ((), (), s32[]{:S(2)}) async-start(), calls=%async_computation.26 | async-start | bytes 1638400 | tf_op jit(solution)/shard_map/all_gather | solution.py:110
  760.5 249.2 %copy-start.208 = (f32[80]{0:T(128)}, f32[80]{0:T(128)S(1)}, u32[]{:S(2)}) copy-start(f32[80]{0:T(128)S(1)} %fusion.196) | copy-start | bytes 964
  817.1 66.2 %all-gather.43.cloned.1.call-start = ((), (), s32[]{:S(2)}) async-start(), calls=%async_computation.41 | async-start | bytes 1638400 | tf_op jit(solution)/shard_map/all_gather | solution.py:118
  817.7 138.0 %reduce-scatter.27.cloned.1.call-start = ((), (), s32[]{:S(2)}) async-start(), calls=%async_computation.31 | async-start | bytes 3276800 | tf_op jit(solution)/shard_map/reduce_scatter | solution.py:122
  904.5 105.2 %reduce-scatter.21.cloned.1.call-start = ((), (), s32[]{:S(2)}) async-start(), calls=%async_computation.27 | async-start | bytes 3276800 | tf_op jit(solution)/shard_map/reduce_scatter | solution.py:114
  911.4 159.1 %all-gather.37.cloned.1.call-start = ((), (), s32[]{:S(2)}) async-start(), calls=%async_computation.29 | async-start | bytes 1638400 | tf_op jit(solution)/shard_map/all_gather | solution.py:118
  1012.8 161.6 %all-gather.39.cloned.1.call-start = ((), (), s32[]{:S(2)}) async-start(), calls=%async_computation.32 | async-start | bytes 1638400 | tf_op jit(solution)/shard_map/all_gather | solution.py:118
  1070.5 628.5 %all-reduce.157.cloned.1.call-start = ((), (), s32[]{:S(2)}) async-start(), calls=%async_computation.42 | async-start | bytes 1310720 | tf_op jit(solution)/shard_map/psum | solution.py:309
  1377.1 100.5 %collective-permute-start.8 = (f32[1,640]{1,0:T(1,128)}, f32[1,640]{1,0:T(1,128)}, u32[]{:S(2)}, u32[]{:S(2)}) collective-permute-start(f32[1,640]{1,0:T(1,128)} %get-tuple-element.78), channel_id=1, source_target_pairs={{4,0},{8,4},{12,8},{5,1},{9,5},{13,9},{6,2},{10,6},{14,10},{7,3},{... | collective-permute-start | bytes 7688 | tf_op jit(solution)/shard_map/ppermute | solution.py:15
  1476.2 6.1 collective-permute-start.12
  1478.2 6.7 collective-permute-start.9
  1482.3 6.4 collective-permute-start.13
  1485.0 52.0 %collective-permute-start.10 = (f32[1,640]{1,0:T(1,128)S(1)}, f32[1,640]{1,0:T(1,128)S(1)}, u32[]{:S(2)}, u32[]{:S(2)}) collective-permute-start(f32[1,640]{1,0:T(1,128)S(1)} %multiply_add_fusion.39), channel_id=1, source_target_pairs={{4,0},{8,4},{12,8},{5,1},{9,5},{13,9},{6,2},{10,6},{14,10},{7,3},{... | collective-permute-start | bytes 7688 | tf_op jit(solution)/shard_map/ppermute | solution.py:15
  1488.7 48.3 %collective-permute-start.14 = (f32[1,640]{1,0:T(1,128)S(1)}, f32[1,640]{1,0:T(1,128)S(1)}, u32[]{:S(2)}, u32[]{:S(2)}) collective-permute-start(f32[1,640]{1,0:T(1,128)S(1)} %multiply_add_fusion.36), channel_id=1, source_target_pairs={{4,0},{8,4},{12,8},{5,1},{9,5},{13,9},{6,2},{10,6},{14,10},{7,3},{... | collective-permute-start | bytes 7688 | tf_op jit(solution)/shard_map/ppermute | solution.py:15
  1557.5 145.3 %reduce-scatter.37.cloned.1.call-start = ((), (), s32[]{:S(2)}) async-start(), calls=%async_computation.37 | async-start | bytes 7077888 | tf_op jit(solution)/shard_map/reduce_scatter | solution.py:293
  1569.1 176.3 %reduce-scatter.39.cloned.1.call-start = ((), (), s32[]{:S(2)}) async-start(), calls=%async_computation.38 | async-start | bytes 7077888 | tf_op jit(solution)/shard_map/reduce_scatter | solution.py:296
  1580.1 230.9 %reduce-scatter.41.cloned.1.call-start = ((), (), s32[]{:S(2)}) async-start(), calls=%async_computation.39 | async-start | bytes 7077888 | tf_op jit(solution)/shard_map/reduce_scatter | solution.py:302
  1591.4 266.4 %reduce-scatter.31.cloned.1.call-start = ((), (), s32[]{:S(2)}) async-start(), calls=%async_computation.34 | async-start | bytes 2949120 | tf_op jit(solution)/shard_map/reduce_scatter | solution.py:287
  1598.9 305.9 %reduce-scatter.35.cloned.1.call-start = ((), (), s32[]{:S(2)}) async-start(), calls=%async_computation.36 | async-start | bytes 2949120 | tf_op jit(solution)/shard_map/reduce_scatter | solution.py:299
  1606.0 345.6 %reduce-scatter.33.cloned.1.call-start = ((), (), s32[]{:S(2)}) async-start(), calls=%async_computation.35 | async-start | bytes 2949120 | tf_op jit(solution)/shard_map/reduce_scatter | solution.py:290
  1631.8 7.3 collective-permute-start.15
  1633.7 8.2 collective-permute-start.11
  1645.1 360.8 %reduce-scatter.25.cloned.1.call-start = ((), (), s32[]{:S(2)}) async-start(), calls=%async_computation.30 | async-start | bytes 3276800 | tf_op jit(solution)/shard_map/reduce_scatter | solution.py:122
  1652.0 408.0 %reduce-scatter.29.cloned.1.call-start = ((), (), s32[]{:S(2)}) async-start(), calls=%async_computation.33 | async-start | bytes 3276800 | tf_op jit(solution)/shard_map/reduce_scatter | solution.py:122
  1658.9 455.2 %reduce-scatter.17.cloned.1.call-start = ((), (), s32[]{:S(2)}) async-start(), calls=%async_computation.23 | async-start | bytes 3276800 | tf_op jit(solution)/shard_map/reduce_scatter | solution.py:114
  (222 other events, 5514.9 us)
Sparse Core Ops, SparseCore 0:
  11.5 35.3 all-gather.16
  48.8 29.0 all-gather.18
  80.1 32.6 all-gather.32
  114.6 29.0 all-gather.20
  145.4 30.5 all-gather.22
  410.3 51.2 reduce-scatter.14
  478.6 52.4 reduce-scatter.18
  533.0 45.1 all-gather.26
  580.3 32.6 all-gather.24
  614.8 44.5 all-gather.28
  661.5 32.6 all-gather.40
  696.0 45.6 all-gather.30
  760.4 52.1 reduce-scatter.22
  817.2 32.3 all-gather.34
  851.6 31.6 all-gather.42
  904.6 51.0 reduce-scatter.26
  957.9 51.7 reduce-scatter.20
  1012.9 32.3 all-gather.36
  1070.6 32.3 all-gather.38
  1557.6 57.4 all-reduce.156
  1618.8 61.1 reduce-scatter.36
  1683.5 61.9 reduce-scatter.38
  1749.2 61.7 reduce-scatter.40
  1814.1 43.6 reduce-scatter.30
  1861.1 43.6 reduce-scatter.34
  1908.0 43.6 reduce-scatter.32
  1953.8 52.0 reduce-scatter.24
  2008.2 51.7 reduce-scatter.28
  2062.3 51.7 reduce-scatter.16
where the time goes:
time: 2200 us; the launch traced here: 2160 us
  waiting for transfers between devices  968 us (44%)
  local copies, waits for them, and re-layouts  614 us (28%)
  other arithmetic  256 us (12%)
  matrix products  200 us (9%)
  blocking collectives  68.4 us (3%)
  starting transfers between devices  40.2 us (2%)
    slice x234, local copies, waits for them, and re-layouts, local_scan(): return lax.associative_scan(combine, (coeffs, offsets), axis=1)  388 us
    reduce_scatter x4, waiting for transfers between devices, narrow_grads(): lax.psum_scatter(partial_vals, 'tensor', scatter_dimension=1, tiled=True)  201 us
    reduce_scatter x4, waiting for transfers between devices, narrow_rows(): lax.psum_scatter(partial_vals, 'tensor', scatter_dimension=1, tiled=True)  151 us
    pad x112, local copies, waits for them, and re-layouts, local_scan(): return lax.associative_scan(combine, (coeffs, offsets), axis=1)  149 us
    all_gather x4, waiting for transfers between devices, widen_rows(): return lax.all_gather(values, 'tensor', axis=1, tiled=True)  127 us
    mul x56, other arithmetic, combine(): return (earlier[0] * following[0], following[0] * earlier[1] + following[1])  76.4 us
    reduce_scatter x1, waiting for transfers between devices, per_device(): lax.psum_scatter(totals[14].astype(jnp.bfloat16), ('fsdp', 'context'), sc...  63.1 us
    dot_general x12, matrix products, project(): jnp.einsum('sla,ab->slb', rows_in, weight, preferred_element_type=jnp.flo...  62.1 us
  transfers between devices with their start and end apart: 45, of which 30 were waited for; matrix products, arithmetic and copies ran while one was open for 36% of the time, Pallas kernels for 0%

commit v1 on v0

--- a/solution.py
+++ b/solution.py
@@ -7,6 +7,27 @@
 CONV = 4
 CPOW = 8
 EPS = 1e-06
+
+
+def collect(array, axis, dim):
+    devices, index, width = (lax.axis_size(axis), lax.axis_index(axis), array.shape[dim])
+    ahead = [(i, (i + 1) % devices) for i in range(devices)]
+    behind = [(i, (i - 1) % devices) for i in range(devices)]
+    out = jnp.zeros((*array.shape[:dim], devices * width, *array.shape[dim + 1 :]), array.dtype)
+    out = lax.dynamic_update_slice_in_dim(out, array, index * width, axis=dim)
+    from_left = from_right = array
+    middle = devices // 2
+    for step in range(1, middle + 1):
+        from_left = lax.ppermute(from_left, axis, ahead)
+        out = lax.dynamic_update_slice_in_dim(
+            out, from_left, (index - step) % devices * width, axis=dim
+        )
+        if step < devices - middle:
+            from_right = lax.ppermute(from_right, axis, behind)
+            out = lax.dynamic_update_slice_in_dim(
+                out, from_right, (index + step) % devices * width, axis=dim
+            )
+    return out
 
 
 def from_behind(value, axis, by):
@@ -107,7 +128,7 @@
 
 
 def widen_rows(values):
-    return lax.all_gather(values, "tensor", axis=1, tiled=True)
+    return collect(values, "tensor", 1)
 
 
 def narrow_rows(partial_vals):

time: 2200 us -> 2060 us (0.936)
  waiting for transfers between devices: 968 us -> 795 us
  starting transfers between devices: 40.2 us -> 76.5 us
    all_gather x4 -> x0, waiting for transfers between devices: 127 us -> none  [widen_rows(): return lax.all_gather(values, 'tensor', axis=1, tiled=True)]
    ppermute x0 -> x12, waiting for transfers between devices: none -> 85.1 us  [the longest x8 50.1 us: collect(): from_left = lax.ppermute(from_left, axis, ahead)]
    all_gather x4, waiting for transfers between devices: 48.6 us -> 0.02 us  [widen_grads(): return lax.all_gather(values, 'tensor', axis=1, tiled=True)]
    ppermute x0 -> x12, starting transfers between devices: none -> 36.7 us  [the longest x8 24.2 us: collect(): from_left = lax.ppermute(from_left, axis, ahead)]
    all_gather x1, waiting for transfers between devices: 31 us -> 0.02 us  [fetch_weights(): lax.all_gather(inner_w, ('fsdp', 'context'), axis=0, tiled=True)]
    reduce_scatter x4, waiting for transfers between devices: 201 us -> 179 us  [narrow_grads(): lax.psum_scatter(partial_vals, 'tensor', scatter_dimension=1, tiled=True)]
  transfers between devices with their start and end apart: 45 -> 53, of which waited for: 30 -> 32; matrix products, arithmetic and copies ran while one was open for 36% -> 44% of each run, Pallas kernels for 0% -> 0%
where the time goes in v1:
time: 2060 us; the launch traced here: 2030 us
  waiting for transfers between devices  795 us (39%)
  local copies, waits for them, and re-layouts  627 us (30%)
  other arithmetic  262 us (13%)
  matrix products  184 us (9%)
  starting transfers between devices  76.5 us (4%)
  blocking collectives  68.4 us (3%)
    slice x234, local copies, waits for them, and re-layouts, local_scan(): return lax.associative_scan(combine, (coeffs, offsets), axis=1)  386 us
    reduce_scatter x4, waiting for transfers between devices, narrow_grads(): lax.psum_scatter(partial_vals, 'tensor', scatter_dimension=1, tiled=True)  179 us
    pad x112, local copies, waits for them, and re-layouts, local_scan(): return lax.associative_scan(combine, (coeffs, offsets), axis=1)  158 us
    reduce_scatter x4, waiting for transfers between devices, narrow_rows(): lax.psum_scatter(partial_vals, 'tensor', scatter_dimension=1, tiled=True)  147 us
    mul x56, other arithmetic, combine(): return (earlier[0] * following[0], following[0] * earlier[1] + following[1])  76.1 us
    reduce_scatter x1, waiting for transfers between devices, per_device(): lax.psum_scatter(totals[14].astype(jnp.bfloat16), ('fsdp', 'context'), sc...  63.1 us
    dot_general x12, matrix products, project(): jnp.einsum('sla,ab->slb', rows_in, weight, preferred_element_type=jnp.flo...  60.9 us
    dot_general x12, matrix products, outer_sum(): jnp.einsum('sla,slb->ab', rows_in, grad_vals, preferred_element_type=jnp....  60.9 us
  transfers between devices with their start and end apart: 53, of which 32 were waited for; matrix products, arithmetic and copies ran while one was open for 44% of the time, Pallas kernels for 0%

profile of v1, /device:TPU:0, one launch (start us, length us, event | category | flops | bytes accessed | tf_op | source)
XLA Modules:
  0.0 2030.8 jit_solution(13684410850203303944)
XLA Ops:
  26.2 5.8 collective-permute-start.2
  31.9 8.3 collective-permute-done.10
  40.3 5.7 collective-permute-start.12
  48.5 5.8 collective-permute-done.2
  570.7 47.8 %reduce-scatter.19.cloned.1.call-done = f32[1,80,2048]{2,1,0:T(8,128)} async-done(((f32[1,320,2048]{2,1,0:T(8,128)}), f32[1,80,2048]{2,1,0:T(8,128)}) %reduce-scatter.19.cloned.1.call-update) | async-done | bytes 655376 | tf_op jit(solution)/shard_map/reduce_scatter | solution.py:135
  628.4 8.8 collective-permute-done.7
  637.2 8.9 collective-permute-start.9
  646.8 10.7 collective-permute-done.8
  658.3 17.4 collective-permute-done.9
  676.4 45.1 %all-gather.23.cloned.1.call-done = bf16[1536,2048]{1,0:T(8,128)(2,1)} async-done(((bf16[1536,256]{1,0:T(8,128)(2,1)}), bf16[1536,2048]{1,0:T(8,128)(2,1)}) %all-gather.23.cloned.1.call-update) | async-done | bytes 6291472 | tf_op jit(solution)/shard_map/all_gather | solution.py:126
  721.5 6.7 fusion.30
  728.2 40.7 %all-gather.21.cloned.1.call-done = bf16[2048,1536]{1,0:T(8,128)(2,1)} async-done(((bf16[256,1536]{1,0:T(8,128)(2,1)}), bf16[2048,1536]{1,0:T(8,128)(2,1)}) %all-gather.21.cloned.1.call-update) | async-done | bytes 6291472 | tf_op jit(solution)/shard_map/all_gather | solution.py:124
  769.0 6.7 fusion.235
  775.6 40.8 %all-gather.19.cloned.1.call-done = bf16[2048,1536]{1,0:T(8,128)(2,1)} async-done(((bf16[256,1536]{1,0:T(8,128)(2,1)}), bf16[2048,1536]{1,0:T(8,128)(2,1)}) %all-gather.19.cloned.1.call-update) | async-done | bytes 6291472 | tf_op jit(solution)/shard_map/all_gather | solution.py:123
  816.4 8.9 multiply_convert_fusion.1
  837.0 24.3 %collective-permute-done.18 = bf16[1,80,2048]{2,1,0:T(8,128)(2,1)S(1)} collective-permute-done((bf16[1,80,2048]{2,1,0:T(8,128)(2,1)}, bf16[1,80,2048]{2,1,0:T(8,128)(2,1)S(1)}, u32[]{:S(2)}, u32[]{:S(2)}) %collective-permute-start.18) | collective-permute-done | bytes 327712 | tf_op jit(solution)/shard_map/ppermute | solution.py:26
  872.0 5.7 fusion.239
  877.8 6.0 multiply_convert_fusion
  889.9 6.9 convolution_bitcast_fusion
  896.8 21.8 %reduce-scatter.23.cloned.1.call-done = f32[1,80,2048]{2,1,0:T(8,128)} async-done(((f32[1,320,2048]{2,1,0:T(8,128)}), f32[1,80,2048]{2,1,0:T(8,128)}) %reduce-scatter.23.cloned.1.call-update) | async-done | bytes 655376 | tf_op jit(solution)/shard_map/reduce_scatter | solution.py:143
  920.5 52.1 %reduce-scatter.27.cloned.1.call-done = f32[1,80,2048]{2,1,0:T(8,128)} async-done(((f32[1,320,2048]{2,1,0:T(8,128)}), f32[1,80,2048]{2,1,0:T(8,128)}) %reduce-scatter.27.cloned.1.call-update) | async-done | bytes 655376 | tf_op jit(solution)/shard_map/reduce_scatter | solution.py:143
  976.5 50.3 %reduce-scatter.21.cloned.1.call-done = f32[1,80,2048]{2,1,0:T(8,128)} async-done(((f32[1,320,2048]{2,1,0:T(8,128)}), f32[1,80,2048]{2,1,0:T(8,128)}) %reduce-scatter.21.cloned.1.call-update) | async-done | bytes 655376 | tf_op jit(solution)/shard_map/reduce_scatter | solution.py:135
  1040.0 5.7 slice.1250
  1045.7 5.6 slice.1259
  1051.3 5.7 slice.1252
  1057.0 5.7 slice.1334
  1068.3 5.6 slice.1336
  1082.0 5.6 slice.1256
  1087.6 5.6 slice.1254
  1175.3 5.6 slice.1340
  1276.3 5.7 slice.1311
  1322.0 5.7 slice.1395
  1364.6 9.5 fusion.244
  1388.9 8.2 rev.19
  1397.1 8.1 rev.20
  1424.0 11.4 add_convert_fusion.2
  1441.5 7.1 add_convert_fusion.1
  1527.5 6.6 convolution_bitcast_fusion.1
  1535.0 28.3 %all-reduce.153 = (bf16[4,640]{1,0:T(4,128)(2,1)S(1)}, bf16[640]{0:T(1024)(128)(2,1)S(1)}, bf16[640]{0:T(1024)(128)(2,1)S(1)}, bf16[640]{0:T(1024)(128)(2,1)S(1)}, bf16[640]{0:T(1024)(128)(2,1)S(1)}) all-reduce(bf16[4,640]{1,0:T(4,128)(2,1)S(1)} %add_convert_fusion.10, ...), channel_id=1, replica_groups=mesh['fsdp'=2,'context'=4,'tensor'=4] {'fsdp','context'}, use_global_device_ids=true, to_apply=%region_29.31 | all-reduce | flops 5120 | bytes 20480 | tf_op jit(solution)/shard_map/psum | solution.py:328
  1572.5 38.8 %reduce-scatter.39.cloned.1.call-done = bf16[256,1536]{1,0:T(8,128)(2,1)} async-done(((bf16[2048,1536]{1,0:T(8,128)(2,1)}), bf16[256,1536]{1,0:T(8,128)(2,1)}) %reduce-scatter.39.cloned.1.call-update) | async-done | bytes 786448 | tf_op jit(solution)/shard_map/reduce_scatter | solution.py:317
  1613.8 63.1 %reduce-scatter.41.cloned.1.call-done = bf16[1536,256]{1,0:T(8,128)(2,1)} async-done(((bf16[1536,2048]{1,0:T(8,128)(2,1)}), bf16[1536,256]{1,0:T(8,128)(2,1)}) %reduce-scatter.41.cloned.1.call-update) | async-done | bytes 786448 | tf_op jit(solution)/shard_map/reduce_scatter | solution.py:323
  1679.3 44.5 %reduce-scatter.31.cloned.1.call-done = bf16[256,640]{1,0:T(8,128)(2,1)} async-done(((bf16[2048,640]{1,0:T(8,128)(2,1)}), bf16[256,640]{1,0:T(8,128)(2,1)}) %reduce-scatter.31.cloned.1.call-update) | async-done | bytes 327696 | tf_op jit(solution)/shard_map/reduce_scatter | solution.py:308
  1725.6 45.1 %reduce-scatter.35.cloned.1.call-done = bf16[640,256]{1,0:T(8,128)(2,1)} async-done(((bf16[640,2048]{1,0:T(8,128)(2,1)}), bf16[640,256]{1,0:T(8,128)(2,1)}) %reduce-scatter.35.cloned.1.call-update) | async-done | bytes 327696 | tf_op jit(solution)/shard_map/reduce_scatter | solution.py:320
  1772.6 45.1 %reduce-scatter.33.cloned.1.call-done = bf16[256,640]{1,0:T(8,128)(2,1)} async-done(((bf16[2048,640]{1,0:T(8,128)(2,1)}), bf16[256,640]{1,0:T(8,128)(2,1)}) %reduce-scatter.33.cloned.1.call-update) | async-done | bytes 327696 | tf_op jit(solution)/shard_map/reduce_scatter | solution.py:311
  1819.5 52.6 %reduce-scatter.25.cloned.1.call-done = f32[1,80,2048]{2,1,0:T(8,128)} async-done(((f32[1,320,2048]{2,1,0:T(8,128)}), f32[1,80,2048]{2,1,0:T(8,128)}) %reduce-scatter.25.cloned.1.call-update) | async-done | bytes 655376 | tf_op jit(solution)/shard_map/reduce_scatter | solution.py:143
  1874.0 52.1 %reduce-scatter.29.cloned.1.call-done = f32[1,80,2048]{2,1,0:T(8,128)} async-done(((f32[1,320,2048]{2,1,0:T(8,128)}), f32[1,80,2048]{2,1,0:T(8,128)}) %reduce-scatter.29.cloned.1.call-update) | async-done | bytes 655376 | tf_op jit(solution)/shard_map/reduce_scatter | solution.py:143
  1931.3 49.0 %reduce-scatter.17.cloned.1.call-done = f32[1,80,2048]{2,1,0:T(8,128)} async-done(((f32[1,320,2048]{2,1,0:T(8,128)}), f32[1,80,2048]{2,1,0:T(8,128)}) %reduce-scatter.17.cloned.1.call-update) | async-done | bytes 655376 | tf_op jit(solution)/shard_map/reduce_scatter | solution.py:135
  1984.1 40.0 %all-reduce.152 = (f32[2048]{0:T(1024)}, f32[2048]{0:T(1024)}) all-reduce(f32[2048]{0:T(1024)S(1)} %add.1533, f32[2048]{0:T(1024)S(1)} %add.1544), channel_id=1, replica_groups=mesh['fsdp'=2,'context'=4,'tensor'=4] {'fsdp','context','tensor'}, use_global_device_ids=true, to_apply=%region_18.20 | all-reduce | flops 4096 | bytes 32768 | tf_op jit(solution)/shard_map/psum | solution.py:336
  (1177 shorter events, 1011.9 us)
Async XLA Ops:
  7.2 53.3 %all-gather.13.cloned.1.call-start = ((), (), s32[]{:S(2)}) async-start(), calls=%async_computation.14 | async-start | bytes 2949120 | tf_op jit(solution)/shard_map/all_gather | solution.py:122
  7.9 66.9 %all-gather.15.cloned.1.call-start = ((), (), s32[]{:S(2)}) async-start(), calls=%async_computation.15 | async-start | bytes 2949120 | tf_op jit(solution)/shard_map/all_gather | solution.py:121
  8.7 419.3 %all-gather.17.cloned.1.call-start = ((), (), s32[]{:S(2)}) async-start(), calls=%async_computation.16 | async-start | bytes 2949120 | tf_op jit(solution)/shard_map/all_gather | solution.py:125
  12.3 13.8 collective-permute-start
  15.3 31.4 %collective-permute-start.1 = (bf16[1,80,2048]{2,1,0:T(8,128)(2,1)}, bf16[1,80,2048]{2,1,0:T(8,128)(2,1)S(1)}, u32[]{:S(2)}, u32[]{:S(2)}) collective-permute-start(bf16[1,80,2048]{2,1,0:T(8,128)(2,1)} %get-tuple-element.124), channel_id=1, source_target_pairs={{0,3},{1,0},{2,1},{3,2},{4,7},{5,4},{6,5},{7,6},{8,11},{9,8},{10,9... | collective-permute-start | bytes 983048 | tf_op jit(solution)/shard_map/ppermute | solution.py:26
  17.4 22.9 %collective-permute-start.10 = (bf16[1,80,2048]{2,1,0:T(8,128)(2,1)}, bf16[1,80,2048]{2,1,0:T(8,128)(2,1)S(1)}, u32[]{:S(2)}, u32[]{:S(2)}) collective-permute-start(bf16[1,80,2048]{2,1,0:T(8,128)(2,1)} %get-tuple-element.125), channel_id=1, source_target_pairs={{0,1},{1,2},{2,3},{3,0},{4,5},{5,6},{6,7},{7,4},{8,9},{9,10},{10,1... | collective-permute-start | bytes 983048 | tf_op jit(solution)/shard_map/ppermute | solution.py:21
  17.4 30.1 %collective-permute-start.11 = (bf16[1,80,2048]{2,1,0:T(8,128)(2,1)}, bf16[1,80,2048]{2,1,0:T(8,128)(2,1)}, u32[]{:S(2)}, u32[]{:S(2)}) collective-permute-start(bf16[1,80,2048]{2,1,0:T(8,128)(2,1)} %get-tuple-element.125), channel_id=1, source_target_pairs={{0,3},{1,0},{2,1},{3,2},{4,7},{5,4},{6,5},{7,6},{8,11},{9,8},{10,9... | collective-permute-start | bytes 983048 | tf_op jit(solution)/shard_map/ppermute | solution.py:26
  21.2 549.5 %reduce-scatter.15.cloned.1.call-start = ((), (), s32[]{:S(2)}) async-start(), calls=%async_computation.17 | async-start | bytes 3276800 | tf_op jit(solution)/shard_map/reduce_scatter | solution.py:135
  26.2 28.1 %collective-permute-start.2 = (bf16[1,80,2048]{2,1,0:T(8,128)(2,1)S(1)}, bf16[1,80,2048]{2,1,0:T(8,128)(2,1)S(1)}, u32[]{:S(2)}, u32[]{:S(2)}) collective-permute-start(bf16[1,80,2048]{2,1,0:T(8,128)(2,1)S(1)} %collective-permute-done), channel_id=1, source_target_pairs={{0,1},{1,2},{2,3},{3,0},{4,5},{5,6},{6,7},{7,4},{8,9},{9,10},{10,1... | collective-permute-start | bytes 983048 | tf_op jit(solution)/shard_map/ppermute | solution.py:21
  40.3 20.2 collective-permute-start.12
  64.4 14.7 collective-permute-start.3
  69.0 10.2 collective-permute-start.13
  357.1 9.7 collective-permute-start.4
  368.2 8.9 collective-permute-start.5
  377.8 46.0 %collective-permute-start.6 = (f32[1,640]{1,0:T(1,128)S(1)}, f32[1,640]{1,0:T(1,128)}, u32[]{:S(2)}, u32[]{:S(2)}) collective-permute-start(f32[1,640]{1,0:T(1,128)S(1)} %multiply_add_fusion.45), channel_id=1, source_target_pairs={{0,4},{4,8},{8,12},{1,5},{5,9},{9,13},{2,6},{6,10},{10,14},{3,7},{... | collective-permute-start | bytes 7688 | tf_op jit(solution)/shard_map/ppermute | solution.py:36
  432.6 185.9 %reduce-scatter.19.cloned.1.call-start = ((), (), s32[]{:S(2)}) async-start(), calls=%async_computation.22 | async-start | bytes 3276800 | tf_op jit(solution)/shard_map/reduce_scatter | solution.py:135
  550.6 8.2 collective-permute-start.16
  565.9 110.5 %all-gather.29.cloned.1.call-start = ((), (), s32[]{:S(2)}) async-start(), calls=%async_computation.36 | async-start | bytes 1638400 | tf_op jit(solution)/shard_map/all_gather | solution.py:139
  567.8 153.7 %all-gather.23.cloned.1.call-start = ((), (), s32[]{:S(2)}) async-start(), calls=%async_computation.20 | async-start | bytes 7077888 | tf_op jit(solution)/shard_map/all_gather | solution.py:126
  568.6 200.4 %all-gather.21.cloned.1.call-start = ((), (), s32[]{:S(2)}) async-start(), calls=%async_computation.19 | async-start | bytes 7077888 | tf_op jit(solution)/shard_map/all_gather | solution.py:124
  569.3 247.1 %all-gather.19.cloned.1.call-start = ((), (), s32[]{:S(2)}) async-start(), calls=%async_computation.18 | async-start | bytes 7077888 | tf_op jit(solution)/shard_map/all_gather | solution.py:123
  570.1 296.3 %all-gather.31.cloned.1.call-start = ((), (), s32[]{:S(2)}) async-start(), calls=%async_computation.37 | async-start | bytes 1638400 | tf_op jit(solution)/shard_map/all_gather | solution.py:139
  570.7 348.0 %reduce-scatter.23.cloned.1.call-start = ((), (), s32[]{:S(2)}) async-start(), calls=%async_computation.24 | async-start | bytes 3276800 | tf_op jit(solution)/shard_map/reduce_scatter | solution.py:143
  622.4 14.8 collective-permute-start.7
  623.0 34.5 %collective-permute-start.8 = (bf16[1,80,2048]{2,1,0:T(8,128)(2,1)S(1)}, bf16[1,80,2048]{2,1,0:T(8,128)(2,1)S(1)}, u32[]{:S(2)}, u32[]{:S(2)}) collective-permute-start(bf16[1,80,2048]{2,1,0:T(8,128)(2,1)S(1)} %get-tuple-element.85), channel_id=1, source_target_pairs={{0,3},{1,0},{2,1},{3,2},{4,7},{5,4},{6,5},{7,6},{8,11},{9,8},{10,9... | collective-permute-start | bytes 983048 | tf_op jit(solution)/shard_map/ppermute | solution.py:26
  628.4 207.7 %collective-permute-start.17 = (bf16[1,80,2048]{2,1,0:T(8,128)(2,1)}, bf16[1,80,2048]{2,1,0:T(8,128)(2,1)S(1)}, u32[]{:S(2)}, u32[]{:S(2)}) collective-permute-start(bf16[1,80,2048]{2,1,0:T(8,128)(2,1)} %get-tuple-element.93), channel_id=1, source_target_pairs={{0,1},{1,2},{2,3},{3,0},{4,5},{5,6},{6,7},{7,4},{8,9},{9,10},{10,1... | collective-permute-start | bytes 983048 | tf_op jit(solution)/shard_map/ppermute | solution.py:21
  637.2 38.5 %collective-permute-start.9 = (bf16[1,80,2048]{2,1,0:T(8,128)(2,1)S(1)}, bf16[1,80,2048]{2,1,0:T(8,128)(2,1)S(1)}, u32[]{:S(2)}, u32[]{:S(2)}) collective-permute-start(bf16[1,80,2048]{2,1,0:T(8,128)(2,1)S(1)} %collective-permute-done.7), channel_id=1, source_target_pairs={{0,1},{1,2},{2,3},{3,0},{4,5},{5,6},{6,7},{7,4},{8,9},{9,10},{10,1... | collective-permute-start | bytes 983048 | tf_op jit(solution)/shard_map/ppermute | solution.py:21
  832.6 140.0 %reduce-scatter.27.cloned.1.call-start = ((), (), s32[]{:S(2)}) async-start(), calls=%async_computation.27 | async-start | bytes 3276800 | tf_op jit(solution)/shard_map/reduce_scatter | solution.py:143
  832.6 28.7 %collective-permute-start.18 = (bf16[1,80,2048]{2,1,0:T(8,128)(2,1)}, bf16[1,80,2048]{2,1,0:T(8,128)(2,1)S(1)}, u32[]{:S(2)}, u32[]{:S(2)}) collective-permute-start(bf16[1,80,2048]{2,1,0:T(8,128)(2,1)} %get-tuple-element.93), channel_id=1, source_target_pairs={{0,3},{1,0},{2,1},{3,2},{4,7},{5,4},{6,5},{7,6},{8,11},{9,8},{10,9... | collective-permute-start | bytes 983048 | tf_op jit(solution)/shard_map/ppermute | solution.py:26
  836.1 29.6 %collective-permute-start.19 = (bf16[1,80,2048]{2,1,0:T(8,128)(2,1)S(1)}, bf16[1,80,2048]{2,1,0:T(8,128)(2,1)S(1)}, u32[]{:S(2)}, u32[]{:S(2)}) collective-permute-start(bf16[1,80,2048]{2,1,0:T(8,128)(2,1)S(1)} %collective-permute-done.17), channel_id=1, source_target_pairs={{0,1},{1,2},{2,3},{3,0},{4,5},{5,6},{6,7},{7,4},{8,9},{9,10},{10,1... | collective-permute-start | bytes 983048 | tf_op jit(solution)/shard_map/ppermute | solution.py:21
  889.8 136.9 %reduce-scatter.21.cloned.1.call-start = ((), (), s32[]{:S(2)}) async-start(), calls=%async_computation.23 | async-start | bytes 3276800 | tf_op jit(solution)/shard_map/reduce_scatter | solution.py:135
  896.8 177.3 %all-gather.25.cloned.1.call-start = ((), (), s32[]{:S(2)}) async-start(), calls=%async_computation.25 | async-start | bytes 1638400 | tf_op jit(solution)/shard_map/all_gather | solution.py:139
  1029.4 137.7 %all-gather.27.cloned.1.call-start = ((), (), s32[]{:S(2)}) async-start(), calls=%async_computation.28 | async-start | bytes 1638400 | tf_op jit(solution)/shard_map/all_gather | solution.py:139
  1074.0 492.4 %all-reduce.157.cloned.1.call-start = ((), (), s32[]{:S(2)}) async-start(), calls=%async_computation.38 | async-start | bytes 1310720 | tf_op jit(solution)/shard_map/psum | solution.py:330
  1305.7 46.3 %collective-permute-start.20 = (f32[1,640]{1,0:T(1,128)}, f32[1,640]{1,0:T(1,128)}, u32[]{:S(2)}, u32[]{:S(2)}) collective-permute-start(f32[1,640]{1,0:T(1,128)} %get-tuple-element.78), channel_id=1, source_target_pairs={{4,0},{8,4},{12,8},{5,1},{9,5},{13,9},{6,2},{10,6},{14,10},{7,3},{... | collective-permute-start | bytes 7688 | tf_op jit(solution)/shard_map/ppermute | solution.py:36
  1359.4 45.8 %collective-permute-start.22 = (f32[1,640]{1,0:T(1,128)S(1)}, f32[1,640]{1,0:T(1,128)S(1)}, u32[]{:S(2)}, u32[]{:S(2)}) collective-permute-start(f32[1,640]{1,0:T(1,128)S(1)} %multiply_add_fusion.39), channel_id=1, source_target_pairs={{4,0},{8,4},{12,8},{5,1},{9,5},{13,9},{6,2},{10,6},{14,10},{7,3},{... | collective-permute-start | bytes 7688 | tf_op jit(solution)/shard_map/ppermute | solution.py:36
  1363.2 42.1 %collective-permute-start.26 = (f32[1,640]{1,0:T(1,128)S(1)}, f32[1,640]{1,0:T(1,128)S(1)}, u32[]{:S(2)}, u32[]{:S(2)}) collective-permute-start(f32[1,640]{1,0:T(1,128)S(1)} %multiply_add_fusion.36), channel_id=1, source_target_pairs={{4,0},{8,4},{12,8},{5,1},{9,5},{13,9},{6,2},{10,6},{14,10},{7,3},{... | collective-permute-start | bytes 7688 | tf_op jit(solution)/shard_map/ppermute | solution.py:36
  1423.7 146.3 %reduce-scatter.37.cloned.1.call-start = ((), (), s32[]{:S(2)}) async-start(), calls=%async_computation.33 | async-start | bytes 7077888 | tf_op jit(solution)/shard_map/reduce_scatter | solution.py:314
  1435.4 175.9 %reduce-scatter.39.cloned.1.call-start = ((), (), s32[]{:S(2)}) async-start(), calls=%async_computation.34 | async-start | bytes 7077888 | tf_op jit(solution)/shard_map/reduce_scatter | solution.py:317
  1448.6 228.2 %reduce-scatter.41.cloned.1.call-start = ((), (), s32[]{:S(2)}) async-start(), calls=%async_computation.35 | async-start | bytes 7077888 | tf_op jit(solution)/shard_map/reduce_scatter | solution.py:323
  1460.4 263.4 %reduce-scatter.31.cloned.1.call-start = ((), (), s32[]{:S(2)}) async-start(), calls=%async_computation.30 | async-start | bytes 2949120 | tf_op jit(solution)/shard_map/reduce_scatter | solution.py:308
  1467.8 302.9 %reduce-scatter.35.cloned.1.call-start = ((), (), s32[]{:S(2)}) async-start(), calls=%async_computation.32 | async-start | bytes 2949120 | tf_op jit(solution)/shard_map/reduce_scatter | solution.py:320
  1474.3 343.4 %reduce-scatter.33.cloned.1.call-start = ((), (), s32[]{:S(2)}) async-start(), calls=%async_computation.31 | async-start | bytes 2949120 | tf_op jit(solution)/shard_map/reduce_scatter | solution.py:311
  1499.3 7.3 collective-permute-start.27
  1501.1 8.1 collective-permute-start.23
  1512.5 359.6 %reduce-scatter.25.cloned.1.call-start = ((), (), s32[]{:S(2)}) async-start(), calls=%async_computation.26 | async-start | bytes 3276800 | tf_op jit(solution)/shard_map/reduce_scatter | solution.py:143
  1519.5 406.6 %reduce-scatter.29.cloned.1.call-start = ((), (), s32[]{:S(2)}) async-start(), calls=%async_computation.29 | async-start | bytes 3276800 | tf_op jit(solution)/shard_map/reduce_scatter | solution.py:143
  1526.3 453.9 %reduce-scatter.17.cloned.1.call-start = ((), (), s32[]{:S(2)}) async-start(), calls=%async_computation.21 | async-start | bytes 3276800 | tf_op jit(solution)/shard_map/reduce_scatter | solution.py:135
  (203 other events, 5990.8 us)
Sparse Core Ops, SparseCore 0:
  9.9 32.8 all-gather.12
  44.7 30.1 all-gather.14
  76.8 30.5 all-gather.16
  432.7 51.2 reduce-scatter.14
  566.0 52.4 reduce-scatter.18
  620.5 54.2 all-gather.28
  676.6 44.8 all-gather.22
  723.4 45.5 all-gather.20
  770.9 45.5 all-gather.18
  818.4 45.2 all-gather.30
  866.0 52.5 reduce-scatter.22
  920.8 51.7 reduce-scatter.26
  974.9 51.7 reduce-scatter.20
  1029.5 32.3 all-gather.24
  1074.1 32.3 all-gather.26
  1423.9 57.4 all-reduce.156
  1485.0 61.1 reduce-scatter.36
  1549.5 61.8 reduce-scatter.38
  1615.1 61.7 reduce-scatter.40
  1680.0 43.6 reduce-scatter.30
  1727.1 43.6 reduce-scatter.34
  1774.0 43.6 reduce-scatter.32
  1820.0 52.0 reduce-scatter.24
  1874.3 51.7 reduce-scatter.28
  1928.4 51.7 reduce-scatter.16
